TPU v7x, 512 devices: a whole 4x4x16 slice. The times are simulated.
512 devices in a mesh: req: 32 (over z, core), mlp: 16 (over y, x).
Axes of the slice: x: 4, y: 4, z: 16, core: 2. Of those that a mesh axis runs over, the one named last changes fastest.
Arguments:
- hidden_input: bfloat16 [12288, 4096], P('req', 'mlp'), may hold values from -6 to 6
- input_norm_gain: bfloat16 [4096], replicated, may hold values from 0.099609375 to 1.8984375
- query_norm_gain: bfloat16 [128], replicated, may hold values from 0.099609375 to 1.8984375
- key_norm_gain: bfloat16 [128], replicated, may hold values from 0.099609375 to 1.8984375
- query_weight: bfloat16 [4096, 4096], P('req', 'mlp'), may hold values from -0.09375 to 0.09375
- key_value_weight: bfloat16 [4096, 2, 1024], P('req'), may hold values from -0.09375 to 0.09375
- output_weight: bfloat16 [4096, 16, 256], P('mlp', None, 'req'), may hold values from -0.09375 to 0.09375
- adapter_down_qkv: bfloat16 [64, 48, 4096], P('req', None, 'mlp'), may hold values from -0.09375 to 0.09375
- adapter_down_output: bfloat16 [64, 16, 4096], P('req', None, 'mlp'), may hold values from -0.09375 to 0.09375
- adapter_up_query: bfloat16 [64, 16, 4096], P('req', None, 'mlp'), may hold values from -1.5 to 1.5
- adapter_up_key_value: bfloat16 [64, 16, 2, 1024], P('req'), may hold values from -1.5 to 1.5
- adapter_up_output: bfloat16 [64, 16, 4096], P('req', None, 'mlp'), may hold values from -1.5 to 1.5
- pool: bfloat16 [16384, 2, 1024], P('req'), may hold values from -6 to 6
- lengths: int32 [32, 4], P('req'), may hold values from 1 to 192, 384 in all within a row
- cached_prefix_pages: int32 [32, 4], P('req'), may hold values from 0 to 8
- prefix_page_table: int32 [32, 4, 8], P('req'), may hold values from 0 to 7, each once within a row
- adapter_of_request: int32 [32, 4, 1], P('req'), may hold values from 0 to 63
- adapter_storage: int32 [64], replicated, may hold values from 0 to 63, each once
Outputs:
- attention_update: bfloat16 [12288, 4096], P('req', 'mlp')
- new_cache: bfloat16 [12288, 2, 1024], P('req', None, 'mlp')
Inputs may be any that keep to these rules, and one draw needn't show every extreme that they name: The lengths of one index of req sum to 384, and the longest of them is 192. `prefix_page_table`: each row lists every page of its pool once. `adapter_of_request`: every adapter is used by some request. `adapter_storage`: each slot holds one adapter.
All inputs are finite; a program needn't handle non-finite values.
Results may differ from a plain program's by a relative error of at most 0.035.
Values may be sent and summed in bfloat16 or wider, within the bound.
A program may use at most 64 MiB of HBM per device.

v0:
```python
import math

import jax
import jax.numpy as jnp
from jax import lax
from jax.sharding import PartitionSpec as P

QUERY_HEADS = 32
KEY_VALUE_HEADS = 8
HEAD_SIZE = 128
ADAPTER_RANK = 16
PAGE = 64


epsilon = 1e-06
rope_base = 1000000.0


def root_mean_scale(values, gain_vec):
    mean_sq = jnp.mean(values * values, axis=-1, keepdims=True)
    return values * lax.rsqrt(mean_sq + epsilon) * gain_vec.astype(jnp.float32)


def rotary_embed(values, token_positions):
    half_width = values.shape[-1] // 2
    inverse_freq = jnp.exp(
        jnp.arange(half_width, dtype=jnp.float32) * (-2.0 / values.shape[-1]) * math.log(rope_base)
    )
    angles = token_positions.astype(jnp.float32)[:, None] * inverse_freq[None, :]
    cosine = jnp.cos(angles)[:, None, :]
    sine_part = jnp.sin(angles)[:, None, :]
    front = values[..., :half_width]
    back = values[..., half_width:]
    return jnp.concatenate(
        [front * cosine - back * sine_part, back * cosine + front * sine_part], axis=-1
    )


def row_tables(lengths_row, prefix_row, page_rows, row_count):
    ends_at = jnp.cumsum(lengths_row)
    starts_at = ends_at - lengths_row
    row_ids = jnp.arange(row_count, dtype=jnp.int32)
    owners = jnp.sum((row_ids[:, None] >= ends_at[None, :]).astype(jnp.int32), axis=1)
    group_members = owners[:, None] == jnp.arange(lengths_row.shape[0], dtype=jnp.int32)[None, :]
    offsets = PAGE * prefix_row[None, :] + row_ids[:, None] - starts_at[None, :]
    token_positions = jnp.sum(jnp.where(group_members, offsets, 0), axis=1)
    page_ids = jnp.arange(page_rows.shape[1], dtype=jnp.int32)
    listed = (page_rows[:, :, None] == page_ids[None, None, :]) & (
        page_ids[None, :, None] < prefix_row[:, None, None]
    )
    page_used = jnp.sum(listed.astype(jnp.float32), axis=1)
    return (owners, group_members, token_positions, page_used)


def apply_adapter(lowrank_inner, group_members, chosen_up):
    masked = lowrank_inner[:, None, :] * group_members.astype(lowrank_inner.dtype)[:, :, None]
    return jnp.einsum("gjr,jrc->gc", masked, chosen_up, preferred_element_type=jnp.float32)


def select_rows(terms, group_members):
    return jnp.sum(terms * group_members.astype(jnp.float32)[:, :, None], axis=1)


def shards(
    hidden_input,
    input_norm_gain,
    query_norm_gain,
    key_norm_gain,
    query_weight,
    key_value_weight,
    output_weight,
    adapter_down_qkv,
    adapter_down_output,
    adapter_up_query,
    adapter_up_key_value,
    adapter_up_output,
    pool,
    lengths,
    cached_prefix_pages,
    prefix_page_table,
    adapter_of_request,
    adapter_storage,
):
    feature_group_count = lax.axis_size("mlp")
    feature_group_index = lax.axis_index("mlp")
    whole = lax.all_gather(hidden_input, "mlp", axis=1, tiled=True)
    row_count, full_width = whole.shape
    normalized_input = root_mean_scale(whole.astype(jnp.float32), input_norm_gain).astype(
        jnp.bfloat16
    )
    owners, group_members, token_positions, page_used = row_tables(
        lengths[0], cached_prefix_pages[0], prefix_page_table[0], row_count
    )
    q_width = query_weight.shape[1]
    query_head_rows = q_width // HEAD_SIZE
    key_value_local = max(1, KEY_VALUE_HEADS // feature_group_count)
    key_value_width = key_value_local * HEAD_SIZE
    key_value_begin = (
        feature_group_index * query_head_rows // (QUERY_HEADS // KEY_VALUE_HEADS) * HEAD_SIZE
    )
    own_wkv = lax.dynamic_slice_in_dim(key_value_weight, key_value_begin, key_value_width, 2)
    request_key_value_up = lax.dynamic_slice_in_dim(
        adapter_up_key_value, key_value_begin, key_value_width, 3
    )
    gathered = (
        lax.all_gather(adapter_down_qkv, "req", axis=0, tiled=True),
        lax.all_gather(adapter_down_output, "req", axis=0, tiled=True),
        lax.all_gather(adapter_up_query, "req", axis=0, tiled=True),
        lax.all_gather(request_key_value_up, "req", axis=0, tiled=True),
        lax.all_gather(adapter_up_output, "req", axis=0, tiled=True),
    )
    slot_indices = jnp.take(adapter_storage, adapter_of_request[0, :, 0], axis=0)
    chosen_down = jnp.take(gathered[0], slot_indices, axis=0)
    output_down = jnp.take(gathered[1], slot_indices, axis=0)
    query_up_part = jnp.take(gathered[2], slot_indices, axis=0)
    key_value_up = jnp.take(gathered[3], slot_indices, axis=0)
    output_up = jnp.take(gathered[4], slot_indices, axis=0)
    feature_cols = full_width // feature_group_count
    own_normed = lax.dynamic_slice_in_dim(
        normalized_input, feature_group_index * feature_cols, feature_cols, 1
    )
    low_terms = jnp.einsum(
        "gd,jkd->gjk", own_normed, chosen_down, preferred_element_type=jnp.float32
    )
    lowrank_inner = lax.psum(select_rows(low_terms, group_members).astype(jnp.bfloat16), "mlp")
    q_part = lax.all_gather(query_weight, "req", axis=0, tiled=True)
    kv_part = lax.all_gather(own_wkv, "req", axis=0, tiled=True)
    query_width_total = jnp.dot(normalized_input, q_part, preferred_element_type=jnp.float32)
    kv_total = jnp.dot(
        normalized_input,
        kv_part.reshape(kv_part.shape[0], 2 * key_value_width),
        preferred_element_type=jnp.float32,
    )
    query_width_total, kv_total = (query_width_total, kv_total)
    query_plain = (
        query_width_total
        + apply_adapter(lowrank_inner[:, 0:ADAPTER_RANK], group_members, query_up_part)
    ).astype(jnp.bfloat16)
    key_lowrank_part = apply_adapter(
        lowrank_inner[:, ADAPTER_RANK : 2 * ADAPTER_RANK], group_members, key_value_up[:, :, 0]
    )
    value_lowrank_part = apply_adapter(
        lowrank_inner[:, 2 * ADAPTER_RANK : 3 * ADAPTER_RANK], group_members, key_value_up[:, :, 1]
    )
    key_value_plain = (
        kv_total.reshape(row_count, 2, key_value_width)
        + jnp.stack([key_lowrank_part, value_lowrank_part], axis=1)
    ).astype(jnp.bfloat16)
    cached = lax.dynamic_slice_in_dim(pool, key_value_begin, key_value_width, 2)
    pool_token_rows = cached.shape[0]
    query_rotated = rotary_embed(
        root_mean_scale(
            query_plain.astype(jnp.float32).reshape(row_count, query_head_rows, HEAD_SIZE),
            query_norm_gain,
        ),
        token_positions,
    ).astype(jnp.bfloat16)
    key_rotated = rotary_embed(
        root_mean_scale(
            key_value_plain[:, 0]
            .astype(jnp.float32)
            .reshape(row_count, key_value_local, HEAD_SIZE),
            key_norm_gain,
        ),
        token_positions,
    ).astype(jnp.bfloat16)
    cache_columns = KEY_VALUE_HEADS * HEAD_SIZE // feature_group_count
    own_offset = feature_group_index * cache_columns - key_value_begin
    local_cache = jnp.stack(
        [key_rotated.reshape(row_count, key_value_width), key_value_plain[:, 1]], axis=1
    )
    new_cache = lax.dynamic_slice_in_dim(local_cache, own_offset, cache_columns, 2)
    key_matrix = jnp.concatenate(
        [cached[:, 0].reshape(pool_token_rows, key_value_local, HEAD_SIZE), key_rotated], axis=0
    )
    value_matrix = jnp.concatenate(
        [
            cached[:, 1].reshape(pool_token_rows, key_value_local, HEAD_SIZE),
            key_value_plain[:, 1].reshape(row_count, key_value_local, HEAD_SIZE),
        ],
        axis=0,
    )
    pool_ok = jnp.dot(group_members.astype(jnp.float32), page_used, precision=lax.Precision.HIGHEST)
    pool_ok = jnp.repeat(pool_ok, PAGE, axis=1) > 0.5
    row_ids = jnp.arange(row_count, dtype=jnp.int32)
    causal = (owners[:, None] == owners[None, :]) & (row_ids[None, :] <= row_ids[:, None])
    allowed = jnp.concatenate([pool_ok, causal], axis=1)
    query_rows = query_rotated.reshape(
        row_count, key_value_local, query_head_rows // key_value_local, HEAD_SIZE
    )
    scores = jnp.einsum(
        "gkhd,skd->khgs", query_rows, key_matrix, preferred_element_type=jnp.float32
    ) / math.sqrt(HEAD_SIZE)
    exp_scores = jnp.where(allowed[None, None], jnp.exp(scores), 0.0)
    softmax = (exp_scores / jnp.sum(exp_scores, axis=-1, keepdims=True)).astype(jnp.bfloat16)
    attended = jnp.einsum(
        "khgs,skd->gkhd", softmax, value_matrix, preferred_element_type=jnp.float32
    )
    attended = attended.astype(jnp.bfloat16).reshape(row_count, q_width)
    out_terms = jnp.einsum("gc,jrc->gjr", attended, output_down, preferred_element_type=jnp.float32)
    lowrank_result = lax.psum(select_rows(out_terms, group_members), "mlp").astype(jnp.bfloat16)
    partial_value = jnp.einsum(
        "gc,cnk->gnk",
        attended,
        lax.all_gather(output_weight, "req", axis=2, tiled=True),
        preferred_element_type=jnp.float32,
    )
    summed_output = lax.psum_scatter(
        partial_value.reshape(row_count, full_width).astype(jnp.bfloat16),
        "mlp",
        scatter_dimension=1,
        tiled=True,
    ).astype(jnp.float32)
    attention_update = (
        summed_output + apply_adapter(lowrank_result, group_members, output_up)
    ).astype(jnp.bfloat16)
    return (attention_update, new_cache)


def solution(mesh):
    return jax.shard_map(
        shards,
        mesh=mesh,
        in_specs=(
            P("req", "mlp"),
            P(),
            P(),
            P(),
            P("req", "mlp"),
            P("req", None, None),
            P("mlp", None, "req"),
            P("req", None, "mlp"),
            P("req", None, "mlp"),
            P("req", None, "mlp"),
            P("req", None, None, None),
            P("req", None, "mlp"),
            P("req", None, None),
            P("req", None),
            P("req", None),
            P("req", None, None),
            P("req", None, None),
            P(),
        ),
        out_specs=(P("req", "mlp"), P("req", None, "mlp")),
        check_vma=False,
    )
```

profile of v0, /device:TPU:32, one launch (start us, length us, event | category | flops | bytes accessed | tf_op | source)
XLA Modules:
  0.0 518.9 jit_solution(2938642543624137017)
XLA Ops:
  7.3 0.7 all-gather.10.cloned.1.call-update
  8.0 0.2 copy-done
  8.2 0.7 constant_dynamic-slice_fusion.2
  9.0 0.7 all-gather.6.cloned.1.call-update
  9.7 0.5 all-gather.12.cloned.1.call-update
  10.3 0.5 all-gather.14.cloned.1.call-update
  10.9 0.7 fusion.90
  11.6 1.3 gather_fusion
  12.9 0.7 fusion.80
  13.5 0.7 compare_and_fusion
  14.2 0.8 reduce-window.4
  15.0 0.7 fusion.81
  15.8 0.6 fusion.76
  16.4 0.1 fusion.28
  16.5 0.7 constant_dynamic-slice_fusion.1
  17.3 36.1 %all_gather.30 = bf16[64,16,2,128]{3,1,2,0:T(8,128)(2,1)S(1)} all-gather(bf16[2,16,2,128]{3,1,2,0:T(8,128)(2,1)S(1)} %copy.66), channel_id=1, replica_groups=mesh['req'=32,'mlp'=16] {'req'}, dimensions={0}, use_global_device_ids=true | all-gather | bytes 540672 | tf_op jit(solution)/shard_map/all_gather | solution.py:109
  53.3 0.7 convert_element_type.100
  54.0 1.2 convert_element_type.109
  55.2 0.7 multiply_bitcast_fusion
  55.9 0.1 select_reduce_fusion
  56.0 1.6 constant_dynamic-slice_fusion
  57.6 30.2 %all_gather.32 = bf16[64,16,256]{2,1,0:T(8,128)(2,1)S(1)} all-gather(bf16[2,16,256]{2,1,0:T(8,128)(2,1)S(1)} %copy-done.6), channel_id=1, replica_groups=mesh['req'=32,'mlp'=16] {'req'}, dimensions={0}, use_global_device_ids=true | all-gather | bytes 540672 | tf_op jit(solution)/shard_map/all_gather | solution.py:108
  87.8 0.5 convert_element_type.112
  88.4 0.1 convert_reduce_fusion
  88.5 0.2 convolution_compare_fusion
  88.7 0.7 copy.65
  89.4 0.6 gather_fusion.2
  90.0 0.7 copy_select_fusion
  90.7 1.2 gather_fusion.3
  91.8 0.8 multiply_cosine_fusion
  92.8 2.6 gather_fusion.1
  95.4 61.2 %all-gather.8.cloned.1.call-done = bf16[4096,2,128]{2,1,0:T(2,128)(2,1)} async-done(((bf16[128,2,128]{2,1,0:T(2,128)(2,1)}), bf16[4096,2,128]{2,1,0:T(2,128)(2,1)}) %all-gather.8.cloned.1.call-update) | async-done | bytes 2097168 | tf_op jit(solution)/shard_map/all_gather | solution.py:127
  156.6 4.7 copy.61
  161.3 63.1 %all-gather.6.cloned.1.call-done = bf16[384,4096]{1,0:T(8,128)(2,1)} async-done(((bf16[384,256]{1,0:T(8,128)(2,1)}), bf16[384,4096]{1,0:T(8,128)(2,1)}) %all-gather.6.cloned.1.call-update) | async-done | bytes 3145744 | tf_op jit(solution)/shard_map/all_gather | solution.py:86
  224.4 2.7 fusion
  227.2 0.1 copy-done.1
  227.3 1.1 fusion.2
  228.4 1.6 copy-done.2
  230.0 0.9 fusion.26
  230.9 72.8 %psum.14 = bf16[384,48]{0,1:T(8,128)(2,1)S(1)} all-reduce(bf16[384,48]{0,1:T(8,128)(2,1)} %fusion.26), channel_id=1, replica_groups=mesh['req'=32,'mlp'=16] {'mlp'}, use_global_device_ids=true, to_apply=%region_4.5 | all-reduce | flops 18432 | bytes 73728 | tf_op jit(solution)/shard_map/psum | solution.py:125
  303.7 0.9 convolution_bitcast_fusion.2
  304.7 0.9 convolution_bitcast_fusion.3
  305.6 3.2 fusion.17
  309.0 0.4 fusion.46
  309.5 0.1 copy.53
  309.6 3.8 fusion.92
  313.5 0.4 multiply_reduce_fusion
  313.8 0.1 copy.54
  314.0 0.1 copy.52
  314.1 0.2 multiply_multiply_fusion
  314.3 0.2 subtract_convert_fusion
  314.5 0.9 fusion.5
  315.5 0.9 fusion.23
  316.4 53.5 %all-gather.14.cloned.1.call-done = bf16[256,16,256]{0,2,1:T(8,128)(2,1)} async-done(((bf16[256,16,8]{0,2,1:T(8,128)(2,1)}), bf16[256,16,256]{0,2,1:T(8,128)(2,1)}) %all-gather.14.cloned.1.call-update) | async-done | bytes 2097168 | tf_op jit(solution)/shard_map/all_gather | solution.py:205
  369.9 4.3 convolution_convert_fusion
  374.2 0.7 copy-done.7
  374.9 28.9 %all_gather.34 = bf16[64,16,256]{2,1,0:T(8,128)(2,1)S(1)} all-gather(bf16[2,16,256]{2,1,0:T(8,128)(2,1)S(1)} %copy-done.7), channel_id=1, replica_groups=mesh['req'=32,'mlp'=16] {'req'}, dimensions={0}, use_global_device_ids=true | all-gather | bytes 540672 | tf_op jit(solution)/shard_map/all_gather | solution.py:107
  403.8 0.5 gather_fusion.4
  404.3 30.1 %all_gather.35 = bf16[64,16,256]{2,1,0:T(8,128)(2,1)S(1)} all-gather(bf16[2,16,256]{2,1,0:T(8,128)(2,1)S(1)} %copy-done.8), channel_id=1, replica_groups=mesh['req'=32,'mlp'=16] {'req'}, dimensions={0}, use_global_device_ids=true | all-gather | bytes 540672 | tf_op jit(solution)/shard_map/all_gather | solution.py:110
  434.4 0.5 gather_fusion.5
  435.0 0.2 fusion.27
  435.2 74.3 %psum.15 = bf16[384,16]{0,1:T(8,128)(2,1)S(1)} all-reduce(f32[384,16]{0,1:T(8,128)S(1)} %fusion.27), channel_id=1, replica_groups=mesh['req'=32,'mlp'=16] {'mlp'}, use_global_device_ids=true, to_apply=%region_12.14 | all-reduce | flops 6144 | bytes 36864 | tf_op jit(solution)/shard_map/psum | solution.py:201
  509.5 0.7 fusion.50
  510.2 1.9 fusion.16
  (62 shorter events, 0.9 us)
Async XLA Ops:
  7.2 1.1 copy-start
  7.2 81.2 %copy-start.17 = (s32[1,4]{1,0:T(1,128)S(1)}, s32[1,4]{1,0:T(1,128)}, u32[]{:S(2)}) copy-start(s32[1,4]{1,0:T(1,128)} %param.34) | copy-start | bytes 52
  7.2 50.4 %copy-start.6 = (bf16[2,16,256]{2,1,0:T(8,128)(2,1)S(1)}, bf16[2,16,256]{2,1,0:T(8,128)(2,1)}, u32[]{:S(2)}) copy-start(bf16[2,16,256]{2,1,0:T(8,128)(2,1)} %param.29) | copy-start | bytes 49156
  7.2 80.6 %copy-start.16 = (bf16[128]{0:T(256)(128)(2,1)S(1)}, bf16[128]{0:T(256)(128)(2,1)}, u32[]{:S(2)}) copy-start(bf16[128]{0:T(256)(128)(2,1)} %param.22) | copy-start | bytes 772
  7.2 81.2 %copy-start.13 = (s32[1,4,8]{2,1,0:T(4,128)S(1)}, s32[1,4,8]{2,1,0:T(4,128)}, u32[]{:S(2)}) copy-start(s32[1,4,8]{2,1,0:T(4,128)} %param.35) | copy-start | bytes 388
  7.2 85.5 %all-gather.10.cloned.1.call-start = ((), (), s32[]{:S(2)}) async-start(), calls=%async_computation.3 | async-start | bytes 1622016 | tf_op jit(solution)/shard_map/all_gather | solution.py:106
  8.0 148.6 %all-gather.8.cloned.1.call-start = ((), (), s32[]{:S(2)}) async-start(), calls=%async_computation.2 | async-start | bytes 2162688 | tf_op jit(solution)/shard_map/all_gather | solution.py:127
  8.9 215.5 %all-gather.6.cloned.1.call-start = ((), (), s32[]{:S(2)}) async-start(), calls=%async_computation.1 | async-start | bytes 3342336 | tf_op jit(solution)/shard_map/all_gather | solution.py:86
  9.7 299.9 %all-gather.12.cloned.1.call-start = ((), (), s32[]{:S(2)}) async-start(), calls=%async_computation.4 | async-start | bytes 2162688 | tf_op jit(solution)/shard_map/all_gather | solution.py:126
  10.3 359.6 %all-gather.14.cloned.1.call-start = ((), (), s32[]{:S(2)}) async-start(), calls=%async_computation.5 | async-start | bytes 2162688 | tf_op jit(solution)/shard_map/all_gather | solution.py:205
  10.8 499.4 %reduce-scatter.2.cloned.1.call-start = ((), (), s32[]{:S(2)}) async-start(), calls=%async_computation.6 | async-start | bytes 3342336 | tf_op jit(solution)/shard_map/reduce_scatter | solution.py:208
  14.2 147.1 %copy-start.11 = (f32[64]{0:T(128)}, f32[64]{0:T(128)S(1)}, u32[]{:S(2)}) copy-start(f32[64]{0:T(128)S(1)} %multiply_exponential_fusion) | copy-start | bytes 772
  224.4 2.8 copy-start.1
  227.3 2.8 copy-start.5
  227.3 2.8 copy-start.9
  228.4 1.7 copy-start.2
  305.6 3.3 copy-start.14
  305.6 3.4 copy-start.12
  309.6 3.9 copy-start.4
  309.6 4.5 copy-start.15
  314.3 1.2 copy-start.3
  374.1 0.7 copy-start.7
  374.1 30.2 %copy-start.8 = (bf16[2,16,256]{2,1,0:T(8,128)(2,1)S(1)}, bf16[2,16,256]{2,1,0:T(8,128)(2,1)}, u32[]{:S(2)}) copy-start(bf16[2,16,256]{2,1,0:T(8,128)(2,1)} %param.31) | copy-start | bytes 49156
  374.1 60.9 %copy-start.10 = (f32[384,4]{0,1:T(4,128)S(1)}, f32[384,4]{0,1:T(4,128)}, u32[]{:S(2)}) copy-start(f32[384,4]{0,1:T(4,128)} %get-tuple-element.17) | copy-start | bytes 18436
Sparse Core Ops, SparseCore 0:
  10.2 75.3 all-gather.9
  87.7 68.8 all-gather.7
  159.6 64.8 all-gather.5
  226.4 71.1 all-gather.11
  299.5 70.3 all-gather.13
  374.3 87.2 reduce-scatter.1
where the time goes:
time: 520 us; the launch traced here: 519 us
  blocking collectives  272 us (52%)
  waiting for transfers between devices  180 us (35%)
  matrix products  18.5 us (4%)
  local copies, waits for them, and re-layouts  18.3 us (4%)
  other arithmetic  14.7 us (3%)
  between operations  14.6 us (3%)
    psum x1, blocking collectives, shards(): lax.psum(select_rows(out_terms, group_members), 'mlp').astype(jnp.bfloat16)  74.3 us
    psum x1, blocking collectives, shards(): lax.psum(select_rows(low_terms, group_members).astype(jnp.bfloat16), 'mlp')  72.8 us
    all_gather x1, waiting for transfers between devices, shards(): whole = lax.all_gather(hidden_input, 'mlp', axis=1, tiled=True)  63.1 us
    all_gather x1, waiting for transfers between devices, shards(): kv_part = lax.all_gather(own_wkv, 'req', axis=0, tiled=True)  61.2 us
    all_gather x1, waiting for transfers between devices, shards(): lax.all_gather(output_weight, 'req', axis=2, tiled=True)  53.5 us
    all_gather x1, blocking collectives, shards(): lax.all_gather(request_key_value_up, 'req', axis=0, tiled=True)  36.1 us
    all_gather x1, blocking collectives, shards(): lax.all_gather(adapter_up_query, 'req', axis=0, tiled=True)  30.2 us
    all_gather x1, blocking collectives, shards(): lax.all_gather(adapter_up_output, 'req', axis=0, tiled=True)  30.1 us
  transfers between devices with their start and end apart: 6, of which 3 were waited for; matrix products, arithmetic and copies ran while one was open for 8% of the time, Pallas kernels for 0%

commit v1 on v0

v1 whole, which is shorter than its diff:
```python
import functools
import math

import jax
import jax.numpy as jnp
from jax import lax
from jax.experimental import pallas as pl
from jax.experimental.pallas import tpu as pltpu
from jax.sharding import PartitionSpec as P

QUERY_HEADS = 32
KEY_VALUE_HEADS = 8
HEAD_SIZE = 128
ADAPTER_RANK = 16
PAGE = 64
MESH = pl.DeviceIdType.MESH

epsilon = 1e-06
rope_base = 1000000.0

Z_COUNT, NX, NY = 16, 4, 4
ROWS, COLS = 384, 256


class Links:
    def __init__(self, send, recv):
        self.send, self.recv, self.used, self.pending = send, recv, 0, []

    def start(self, src, dst, device):
        slot = self.used
        self.used += 1
        copy = pltpu.make_async_remote_copy(
            src_ref=src,
            dst_ref=dst,
            send_sem=self.send.at[slot],
            recv_sem=self.recv.at[slot],
            device_id=device,
            device_id_type=MESH,
        )
        copy.start()
        self.pending.append(copy)
        return copy

    def drain(self):
        for copy in self.pending:
            copy.wait_send()
        self.pending = []


class Place:
    def __init__(self):
        self.r = lax.axis_index("req")
        self.m = lax.axis_index("mlp")
        self.x = lax.rem(self.m, NX)
        self.y = lax.div(self.m, NX)

    def along(self, axis, step):
        if axis == "x":
            return self.m - self.x + lax.rem(self.x + (step + NX), NX)
        return lax.rem(self.m + (step + NY) * NX, NX * NY)

    def at(self, axis_a, i, axis_b, j):
        x = self.x + (i if axis_a == "x" else j) + NX
        y = self.y + (i if axis_a == "y" else j) + NY
        return lax.rem(y, NY) * NX + lax.rem(x, NX)


def barrier(place, whole_plane):
    sem = pltpu.get_barrier_semaphore()
    n = 0
    r, m = place.r, place.m
    for other in (lax.rem(r + 2, 32), lax.rem(r + 30, 32), r + 1 - 2 * lax.rem(r, 2)):
        pl.semaphore_signal(sem, inc=1, device_id=(other, m), device_id_type=MESH)
        n += 1
    for d in range(1, NX * NY):
        other = lax.rem(m + d, NX * NY)
        pl.semaphore_signal(sem, inc=1, device_id=(r, other), device_id_type=MESH)
        n += 1
    pl.semaphore_wait(sem, n)


class PlaneGather:
    def __init__(self, links, place, buf, rows):
        self.links, self.place, self.buf, self.rows = links, place, buf, rows
        self.p1, self.p2, self.q1, self.q2 = {}, {}, {}, {}
        self.axes = [("x", "y"), ("y", "x")]

    def view(self, h, piece, part=None):
        rows = self.rows // 2
        begin = h * rows
        if part is not None:
            rows //= 2
            begin += part * rows
        return self.buf.at[piece, pl.ds(begin, rows), :]

    def send(self, h, axis, step, piece, part=None):
        view = self.view(h, piece, part)
        return self.links.start(view, view, (self.place.r, self.place.along(axis, step)))

    def piece(self, h, i):
        a, b = self.axes[h]
        return self.place.at(a, i, b, 0)

    def start_second(self, h, i):
        b = self.axes[h][1]
        for s in (1, -1):
            self.q1[h, i, s] = self.send(h, b, s, self.piece(h, i))

    def e0(self):
        for h in range(2):
            a = self.axes[h][0]
            for s in (1, -1):
                self.p1[h, s] = self.send(h, a, s, self.place.m)
        for h in range(2):
            self.start_second(h, 0)

    def e1(self):
        for h in range(2):
            a = self.axes[h][0]
            for s in (1, -1):
                self.p1[h, s].wait_recv()
                self.p2[h, s] = self.send(h, a, s, self.piece(h, -s), 0 if s == 1 else 1)
        for h in range(2):
            for s in (1, -1):
                self.start_second(h, -s)

    def e2(self):
        for h in range(2):
            for s in (1, -1):
                self.p2[h, s].wait_recv()
            self.start_second(h, 2)

    def e3(self, i):
        for h in range(2):
            a, b = self.axes[h]
            for s in (1, -1):
                self.q1[h, i, s].wait_recv()
                piece = self.place.at(a, i, b, -s)
                self.q2[h, i, s] = self.send(h, b, s, piece, 0 if s == 1 else 1)

    def e4(self):
        for copy in self.q2.values():
            copy.wait_recv()

    def run(self):
        self.e0()
        self.e1()
        self.e2()
        for i in (0, -1, 1, 2):
            self.e3(i)
        self.e4()


class RingGather:
    def __init__(self, links, place, view, halves):
        self.links, self.place, self.view, self.halves = links, place, view, halves
        self.z, self.sib = {}, []

    def shard(self, t):
        return lax.rem(self.place.r + (2 * t + 32), 32)

    def send(self, t, s):
        shard = self.shard(-s * t)
        target = (lax.rem(self.place.r + (2 * s + 32), 32), self.place.m)
        if t == Z_COUNT // 2 - 1:
            view = self.halves(shard, 0 if s == 1 else 1)
        else:
            view = self.view(shard)
        self.z[t, s] = self.links.start(view, view, target)

    def sibling(self, t):
        view = self.view(self.shard(t))
        r = self.place.r
        self.sib.append(
            self.links.start(view, view, (r + 1 - 2 * lax.rem(r, 2), self.place.m))
        )

    def step(self, t):
        last = Z_COUNT // 2
        if t == 0:
            for s in (1, -1):
                self.send(0, s)
            self.sibling(0)
            return
        for s in (1, -1):
            self.z[t - 1, s].wait_recv()
            if t < last:
                self.send(t, s)
        if t < last:
            for s in (1, -1):
                self.sibling(-s * t)
        else:
            self.sibling(last)

    def finish(self):
        for copy in self.sib:
            copy.wait_recv()


def halves_of(ref, rows):
    return (
        lambda shard: ref.at[shard],
        lambda shard, part: ref.at[shard, pl.ds(part * (rows // 2), rows // 2), :],
    )


def gather_kernel(
    lengths,
    chosen,
    storage,
    hid,
    gain,
    down_qkv,
    wq,
    wkv,
    up_q,
    up_kv,
    down_out,
    up_out,
    wo,
    hid_all,
    mid_all,
    late_all,
    wo_all,
    low_out,
    down_all,
    low_all,
    send,
    recv,
    local,
):
    place = Place()
    r, m = place.r, place.m
    links = Links(send, recv)

    staged = []

    def stage(src, dst):
        copy = pltpu.make_async_copy(src, dst, local.at[len(staged)])
        copy.start()
        staged.append(copy)

    for i in range(2):
        stage(down_qkv.at[i], down_all.at[r, pl.ds(48 * i, 48), :])
    stage(hid, hid_all.at[m])
    stage(wq, mid_all.at[r, pl.ds(0, 128), :])
    stage(wkv, mid_all.at[r, pl.ds(128, 128), :])
    for i in range(2):
        stage(up_q.at[i], mid_all.at[r, pl.ds(256 + 16 * i, 16), :])
        stage(up_kv.at[i], mid_all.at[r, pl.ds(288 + 16 * i, 16), :])
        stage(down_out.at[i], late_all.at[r, pl.ds(16 * i, 16), :])
        stage(up_out.at[i], late_all.at[r, pl.ds(32 + 16 * i, 16), :])
    stage(wo.at[m], wo_all.at[m, pl.ds(r * 8, 8), :])
    barrier(place, True)
    for copy in staged:
        copy.wait()

    plane = PlaneGather(links, place, hid_all, ROWS)
    early = RingGather(links, place, *halves_of(down_all, 96))
    mid = RingGather(links, place, *halves_of(mid_all, 320))
    late = RingGather(links, place, *halves_of(late_all, 64))
    out = RingGather(
        links,
        place,
        lambda shard: wo_all.at[:, pl.ds(shard * 8, 8), :],
        lambda shard, part: wo_all.at[pl.ds(8 * part, 8), pl.ds(shard * 8, 8), :],
    )

    early.step(0)
    plane.e0()
    mid.step(0)
    swaps = []
    for d in range(1, 16):
        other = lax.rem(m + d, 16)
        swaps.append(links.start(wo.at[other], wo_all.at[m, pl.ds(r * 8, 8), :], (r, other)))
    early.step(1)
    plane.e1()
    mid.step(1)
    early.step(2)
    plane.e2()
    mid.step(2)
    for copy in swaps:
        copy.wait_recv()
    early.step(3)
    plane.e3(0)
    mid.step(3)
    early.step(4)
    late.step(0)
    out.step(0)
    plane.e3(-1)
    mid.step(4)
    early.step(5)
    plane.e3(1)
    mid.step(5)
    early.step(6)
    plane.e3(2)
    mid.step(6)
    early.step(7)
    mid.step(7)
    early.step(8)
    early.finish()

    e1 = lengths[0, 0]
    e2 = e1 + lengths[0, 1]
    e3 = e2 + lengths[0, 2]
    token = lax.broadcasted_iota(jnp.int32, (1, ROWS), 1)
    owner = (
        (token >= e1).astype(jnp.int32)
        + (token >= e2).astype(jnp.int32)
        + (token >= e3).astype(jnp.int32)
    )
    scaled = (hid[...].astype(jnp.float32) * gain[...]).astype(jnp.bfloat16)
    low = jnp.zeros((48, ROWS), jnp.float32)
    for j in range(4):
        slot = storage[chosen[0, j]]
        down = down_all[slot // 2, pl.ds((slot % 2) * 48, 48), :]
        terms = lax.dot_general(
            down, scaled, (((1,), (1,)), ((), ())), preferred_element_type=jnp.float32
        )
        low = low + jnp.where(owner == j, terms, 0.0)
    low_all[m, 0:48, :] = low.astype(jnp.bfloat16)
    low_all[m, 48:64, :] = jnp.zeros((16, ROWS), jnp.bfloat16)
    lows = PlaneGather(links, place, low_all, 64)
    lows.e0()
    mid.step(8)
    lows.e1()
    late.step(1)
    out.step(1)
    lows.e2()
    late.step(2)
    out.step(2)
    for i in (0, -1, 1, 2):
        lows.e3(i)
    for t in range(3, 9):
        late.step(t)
        out.step(t)
    lows.e4()
    total = jnp.zeros((64, ROWS), jnp.float32)
    for i in range(16):
        total = total + low_all[i].astype(jnp.float32)
    low_out[...] = total
    plane.e4()
    mid.finish()
    late.finish()
    out.finish()
    links.drain()


def gather_attended_kernel(att, low, att_all, low_all, send, recv, local):
    place = Place()
    links = Links(send, recv)
    a = pltpu.make_async_copy(att, att_all.at[place.m], local.at[0])
    b = pltpu.make_async_copy(low, low_all.at[place.m], local.at[1])
    a.start()
    b.start()
    barrier(place, False)
    a.wait()
    b.wait()
    plane = PlaneGather(links, place, att_all, ROWS)
    lows = PlaneGather(links, place, low_all, 32)
    lows.e0()
    plane.e0()
    lows.e1()
    plane.e1()
    lows.e2()
    plane.e2()
    for i in (0, -1, 1, 2):
        lows.e3(i)
        plane.e3(i)
    lows.e4()
    plane.e4()
    links.drain()


def rotary_tables(token_positions, width):
    half_width = width // 2
    inverse_freq = jnp.exp(
        jnp.arange(half_width, dtype=jnp.float32) * (-2.0 / width) * math.log(rope_base)
    )
    angles = token_positions.astype(jnp.float32)[:, None] * inverse_freq[None, :]
    return jnp.cos(angles)[:, None, :], jnp.sin(angles)[:, None, :]


def head_norm_rotate(values, gain_vec, cosine, sine_part):
    mean_sq = jnp.mean(values * values, axis=-1, keepdims=True)
    values = values * lax.rsqrt(mean_sq + epsilon) * gain_vec.astype(jnp.float32)
    half_width = values.shape[-1] // 2
    front = values[..., :half_width]
    back = values[..., half_width:]
    return jnp.concatenate(
        [front * cosine - back * sine_part, back * cosine + front * sine_part], axis=-1
    )


def row_tables(lengths_row, prefix_row, page_rows, row_count):
    ends_at = jnp.cumsum(lengths_row)
    starts_at = ends_at - lengths_row
    row_ids = jnp.arange(row_count, dtype=jnp.int32)
    owners = jnp.sum((row_ids[:, None] >= ends_at[None, :]).astype(jnp.int32), axis=1)
    group_members = owners[:, None] == jnp.arange(lengths_row.shape[0], dtype=jnp.int32)[None, :]
    offsets = PAGE * prefix_row[None, :] + row_ids[:, None] - starts_at[None, :]
    token_positions = jnp.sum(jnp.where(group_members, offsets, 0), axis=1)
    page_ids = jnp.arange(page_rows.shape[1], dtype=jnp.int32)
    listed = (page_rows[:, :, None] == page_ids[None, None, :]) & (
        page_ids[None, :, None] < prefix_row[:, None, None]
    )
    page_used = jnp.sum(listed.astype(jnp.float32), axis=1)
    return (owners, group_members, token_positions, page_used)


def apply_adapter(lowrank_inner, group_members, chosen_up):
    masked = lowrank_inner[:, None, :] * group_members.astype(lowrank_inner.dtype)[:, :, None]
    return jnp.einsum("gjr,jrc->gc", masked, chosen_up, preferred_element_type=jnp.float32)


def shards(
    hidden_input,
    input_norm_gain,
    query_norm_gain,
    key_norm_gain,
    query_weight,
    key_value_weight,
    output_weight,
    adapter_down_qkv,
    adapter_down_output,
    adapter_up_query,
    adapter_up_key_value,
    adapter_up_output,
    pool,
    lengths,
    cached_prefix_pages,
    prefix_page_table,
    adapter_of_request,
    adapter_storage,
):
    mi = lax.axis_index("mlp")
    begin = mi // 2 * HEAD_SIZE
    bf16 = jnp.bfloat16
    own_wkv = lax.dynamic_slice_in_dim(key_value_weight, begin, HEAD_SIZE, 2).reshape(128, 256)
    own_ukv = lax.dynamic_slice_in_dim(adapter_up_key_value, begin, HEAD_SIZE, 3).reshape(2, 16, 256)
    cached = lax.dynamic_slice_in_dim(pool, begin, HEAD_SIZE, 2)
    gain_rows = input_norm_gain.astype(jnp.float32).reshape(16, 1, COLS)
    gain_own = lax.dynamic_slice_in_dim(gain_rows, mi, 1, 0).reshape(1, COLS)
    wo_local = jnp.transpose(output_weight, (1, 2, 0))

    smem = pl.BlockSpec(memory_space=pltpu.SMEM)
    vmem = pl.BlockSpec(memory_space=pltpu.VMEM)
    hbm = pl.BlockSpec(memory_space=pl.ANY)
    sems = 400
    hid_all, mid_all, late_all, wo_all, low = pl.pallas_call(
        gather_kernel,
        out_shape=(
            jax.ShapeDtypeStruct((16, ROWS, COLS), bf16),
            jax.ShapeDtypeStruct((32, 320, COLS), bf16),
            jax.ShapeDtypeStruct((32, 64, COLS), bf16),
            jax.ShapeDtypeStruct((16, 256, COLS), bf16),
            jax.ShapeDtypeStruct((64, ROWS), jnp.float32),
        ),
        in_specs=[smem] * 3 + [vmem] * 2 + [hbm] * 8,
        out_specs=(hbm, hbm, hbm, hbm, vmem),
        scratch_shapes=[
            pltpu.VMEM((32, 96, COLS), bf16),
            pltpu.VMEM((16, 64, ROWS), bf16),
            pltpu.SemaphoreType.DMA((sems,)),
            pltpu.SemaphoreType.DMA((sems,)),
            pltpu.SemaphoreType.DMA((16,)),
        ],
        compiler_params=pltpu.CompilerParams(collective_id=0, has_side_effects=True),
        name="gather",
    )(
        lengths,
        adapter_of_request.reshape(1, 4),
        adapter_storage,
        hidden_input,
        gain_own,
        adapter_down_qkv,
        query_weight,
        own_wkv,
        adapter_up_query,
        own_ukv,
        adapter_down_output,
        adapter_up_output,
        wo_local,
    )

    row_count = ROWS
    owners, group_members, token_positions, page_used = row_tables(
        lengths[0], cached_prefix_pages[0], prefix_page_table[0], row_count
    )
    slot_indices = jnp.take(adapter_storage, adapter_of_request[0, :, 0], axis=0)
    hid32 = hid_all.astype(jnp.float32)
    scale = lax.rsqrt(jnp.sum(hid32 * hid32, axis=(0, 2)) / 4096.0 + epsilon)[:, None]
    scaled = (hid32 * gain_rows).astype(bf16)
    weights = mid_all[:, 0:256].reshape(16, 2, 2, 128, 256)
    weights = jnp.transpose(weights, (0, 1, 3, 2, 4)).reshape(4096, 512)
    wide = jnp.transpose(scaled, (1, 0, 2)).reshape(ROWS, 4096)
    total = jnp.dot(wide, weights, preferred_element_type=jnp.float32)
    low_t = low.T.astype(bf16)
    ups_q = jnp.take(mid_all[:, 256:288].reshape(64, 16, 256), slot_indices, axis=0)
    ups_kv = jnp.take(mid_all[:, 288:320].reshape(64, 16, 256), slot_indices, axis=0)
    query_plain = (
        scale * (total[:, 0:256] + apply_adapter(low_t[:, 0:16], group_members, ups_q))
    ).astype(bf16)
    key_plain = (
        scale
        * (total[:, 256:384] + apply_adapter(low_t[:, 16:32], group_members, ups_kv[:, :, 0:128]))
    ).astype(bf16)
    value_plain = (
        scale
        * (total[:, 384:512] + apply_adapter(low_t[:, 32:48], group_members, ups_kv[:, :, 128:]))
    ).astype(bf16)
    cosine, sine_part = rotary_tables(token_positions, HEAD_SIZE)
    query_rotated = head_norm_rotate(
        query_plain.astype(jnp.float32).reshape(row_count, 2, HEAD_SIZE),
        query_norm_gain,
        cosine,
        sine_part,
    ).astype(bf16)
    key_rotated = head_norm_rotate(
        key_plain.astype(jnp.float32).reshape(row_count, 1, HEAD_SIZE),
        key_norm_gain,
        cosine,
        sine_part,
    ).astype(bf16)[:, 0]
    local_cache = jnp.stack([key_rotated, value_plain], axis=1)
    new_cache = lax.dynamic_slice_in_dim(local_cache, mi % 2 * 64, 64, 2)
    key_matrix = jnp.concatenate([cached[:, 0], key_rotated], axis=0)
    value_matrix = jnp.concatenate([cached[:, 1], value_plain], axis=0)
    pool_ok = jnp.dot(group_members.astype(jnp.float32), page_used, precision=lax.Precision.HIGHEST)
    pool_ok = jnp.repeat(pool_ok, PAGE, axis=1) > 0.5
    row_ids = jnp.arange(row_count, dtype=jnp.int32)
    causal = (owners[:, None] == owners[None, :]) & (row_ids[None, :] <= row_ids[:, None])
    allowed = jnp.concatenate([pool_ok, causal], axis=1)
    scores = jnp.einsum(
        "ghd,sd->hgs", query_rotated, key_matrix, preferred_element_type=jnp.float32
    ) / math.sqrt(HEAD_SIZE)
    exp_scores = jnp.where(allowed[None], jnp.exp(scores), 0.0)
    softmax = (exp_scores / jnp.sum(exp_scores, axis=-1, keepdims=True)).astype(bf16)
    attended = jnp.einsum("hgs,sd->ghd", softmax, value_matrix, preferred_element_type=jnp.float32)
    attended = attended.astype(bf16).reshape(row_count, COLS)
    downs = jnp.take(late_all[:, 0:32].reshape(64, 16, 256), slot_indices, axis=0)
    terms = jnp.einsum("jrc,gc->jrg", downs, attended, preferred_element_type=jnp.float32)
    low_part = jnp.sum(terms * group_members.astype(jnp.float32).T[:, None, :], axis=0)
    low_part = jnp.pad(low_part.astype(bf16), ((0, 16), (0, 0)))
    att_all, low_all = pl.pallas_call(
        gather_attended_kernel,
        out_shape=(
            jax.ShapeDtypeStruct((16, ROWS, COLS), bf16),
            jax.ShapeDtypeStruct((16, 32, ROWS), bf16),
        ),
        in_specs=[hbm] * 2,
        out_specs=(hbm, hbm),
        scratch_shapes=[
            pltpu.SemaphoreType.DMA((80,)),
            pltpu.SemaphoreType.DMA((80,)),
            pltpu.SemaphoreType.DMA((2,)),
        ],
        compiler_params=pltpu.CompilerParams(collective_id=1, has_side_effects=True),
        name="gather_attended",
    )(attended, low_part)
    ups_out = jnp.take(late_all[:, 32:64].reshape(64, 16, 256), slot_indices, axis=0)
    low_sum = jnp.sum(low_all[:, 0:16].astype(jnp.float32), axis=0).T.astype(bf16)
    update = jnp.einsum("mgk,mck->gc", att_all, wo_all, preferred_element_type=jnp.float32)
    attention_update = (update + apply_adapter(low_sum, group_members, ups_out)).astype(bf16)
    return (attention_update, new_cache)


def solution(mesh):
    return jax.shard_map(
        shards,
        mesh=mesh,
        in_specs=(
            P("req", "mlp"),
            P(),
            P(),
            P(),
            P("req", "mlp"),
            P("req", None, None),
            P("mlp", None, "req"),
            P("req", None, "mlp"),
            P("req", None, "mlp"),
            P("req", None, "mlp"),
            P("req", None, None, None),
            P("req", None, "mlp"),
            P("req", None, None),
            P("req", None),
            P("req", None),
            P("req", None, None),
            P("req", None, None),
            P(),
        ),
        out_specs=(P("req", "mlp"), P("req", None, "mlp")),
        check_vma=False,
    )
```

time: 520 us -> 201 us (0.39)
  the two profiles are of different devices: /device:TPU:32 before, /device:TPU:1 now
where the time goes in v1:
time: 201 us; the launch traced here: 200 us
  Pallas kernels  135 us (67%)
  local copies, waits for them, and re-layouts  30.8 us (15%)
  other arithmetic  20.1 us (10%)
  matrix products  12.6 us (6%)
    pallas_call x1, Pallas kernels, shards(): pl.pallas_call(gather_kernel, out_shape=(jax.ShapeDtypeStruct((16, ROWS,...  103 us
    pallas_call x1, Pallas kernels, shards(): pl.pallas_call(gather_attended_kernel, out_shape=(jax.ShapeDtypeStruct((1...  32.2 us
    reshape x1, local copies, waits for them, and re-layouts, shards(): weights = mid_all[:, 0:256].reshape(16, 2, 2, 128, 256)  6.54 us
    unnamed x33, local copies, waits for them, and re-layouts  6.33 us
    reduce_sum x1, other arithmetic, shards(): jnp.sum(hid32 * hid32, axis=(0, 2)) / 4096.0 + epsilon  5.97 us
    dot_general x1, matrix products, shards(): total = jnp.dot(wide, weights, preferred_element_type=jnp.float32)  4.96 us
    transpose x1, local copies, waits for them, and re-layouts, shards(): wide = jnp.transpose(scaled, (1, 0, 2)).reshape(ROWS, 4096)  4.66 us

profile of v1, /device:TPU:1, one launch (start us, length us, event | category | flops | bytes accessed | tf_op | source)
XLA Modules:
  0.0 200.0 jit_solution(13511998826173233569)
XLA Ops:
  0.6 0.0 copy-start
  0.7 0.9 reduce-window.4
  1.6 1.2 convert_element_type.113
  2.8 1.2 convert_element_type.110
  4.1 0.7 iota_compare_fusion.6
  4.8 0.7 fusion.68
  5.4 0.7 fusion.69
  6.1 0.8 convert_reduce_fusion
  6.9 0.1 convert_reduce_fusion.1
  7.0 0.1 select_reduce_fusion
  7.1 0.2 convolution_compare_fusion
  7.3 1.3 gather_fusion
  8.6 1.1 compare_and_fusion
  9.7 0.6 pad_clamp_fusion
  10.3 0.7 constant_dynamic-slice_fusion.1
  11.1 0.6 reshape.349.up_kv
  11.7 0.7 mul.230
  12.4 0.7 convert_element_type.99
  13.1 0.5 fusion.67.gain
  13.7 0.6 copy.96
  14.3 0.1 fusion.20
  14.4 0.1 broadcast_in_dim.25
  14.5 0.8 pad_add_fusion
  15.3 0.8 multiply_cosine_fusion
  16.1 1.6 constant_dynamic-slice_fusion
  17.7 0.7 copy_bitcast_fusion
  18.5 103.2 %gather.26 = (bf16[16,384,256]{2,1,0:T(8,128)(2,1)}, bf16[32,320,256]{2,1,0:T(8,128)(2,1)}, bf16[32,64,256]{2,1,0:T(8,128)(2,1)}, bf16[16,256,256]{2,1,0:T(8,128)(2,1)}, f32[64,384]{1,0:T(8,128)}) custom-call(s32[1,4]{1,0:T(1,128)} %lengths.1, s32[1,4]{1,0:T(1,128)} %bitcast.147, s32[64]{0:T(128)} %storage.1, bf16[384,256]{1,0:T(8,128)(2,1)} %hid.1, ...), custom_call_target="tpu_custom_call" | custom-call | tf_op jit(solution)/shard_map/gather/pallas_call | solution.py:450
  121.7 6.0 %fusion = (f32[384]{0:T(512)S(1)}, bf16[384,16,256]{2,0,1:T(8,128)(2,1)}) fusion(bf16[16,384,256]{2,1,0:T(8,128)(2,1)} %get-tuple-element.10, f32[16,256]{1,0:T(8,128)S(1)} %mul.230), kind=kLoop, calls=%fused_computation.7 | loop fusion | flops 7863936 | bytes 6309376 | tf_op jit(solution)/shard_map/reduce_sum | solution.py:492
  127.7 0.6 add_rsqrt_fusion.2
  128.3 0.9 convert_bitcast_fusion
  129.2 0.6 fusion.79
  129.8 1.0 fusion.77
  130.8 0.4 slice.61
  131.2 6.5 %copy.66 = bf16[16,2,2,128,256]{4,2,3,1,0:T(2,128)(2,1)} copy(bf16[16,2,2,128,256]{4,3,2,1,0:T(8,128)(2,1)S(1)} %bitcast.127) | data formatting | bytes 8388608 | tf_op jit(solution)/shard_map/reshape | solution.py:494
  137.8 4.8 %copy.91 = bf16[512,8,2,256]{3,1,2,0:T(8,128)(2,1)} copy(bf16[512,8,2,256]{3,2,1,0:T(2,128)(2,1)} %bitcast.128) | data formatting | bytes 8388608
  142.6 1.6 gather_fusion.2
  144.2 0.5 gather_fusion.1
  144.8 0.1 broadcast_select_fusion
  144.8 0.5 gather_fusion.3
  145.4 0.5 gather_fusion.4
  146.0 4.7 %copy.65 = bf16[384,16,256]{0,2,1:T(8,128)(2,1)} copy(bf16[384,16,256]{2,0,1:T(8,128)(2,1)} %get-tuple-element.32) | data formatting | bytes 6291456 | tf_op jit(solution)/shard_map/transpose | solution.py:496
  150.6 5.0 %fusion.80 = f32[384,512]{1,0:T(8,128)S(1)} fusion(bf16[384,4096]{0,1:T(8,128)(2,1)} %bitcast.130, bf16[4096,512]{1,0:T(8,128)(2,1)} %bitcast.129), kind=kOutput, calls=%fused_computation.144 | convolution fusion | flops 1610612736 | bytes 8126464 | tf_op jit(solution)/shard_map/dot_general | solution.py:497
  155.6 0.2 fusion.17
  155.9 0.3 multiply_reduce_fusion.1
  156.2 0.0 copy-start.5
  156.2 0.3 fusion.11
  156.5 0.1 multiply_bitcast_fusion
  156.7 0.8 fusion.34
  157.5 0.2 dynamic-slice_maximum_fusion
  157.7 0.8 copy.75
  158.4 0.2 reshape.363
  158.6 0.5 multiply_reduce_fusion
  159.1 0.1 copy.70
  159.2 0.0 copy-done.14
  159.3 0.2 fusion.21
  159.4 0.2 subtract_convert_fusion
  159.7 0.9 fusion.3
  160.6 0.9 fusion.9
  161.5 0.2 fusion.19
  161.8 0.8 copy.85.att
  162.6 0.6 pad.4.low
  163.2 32.2 %gather_attended.1 = (bf16[16,384,256]{2,1,0:T(8,128)(2,1)}, bf16[16,32,384]{2,1,0:T(8,128)(2,1)}) custom-call(bf16[384,256]{1,0:T(8,128)(2,1)} %copy.85.att, bf16[32,384]{1,0:T(8,128)(2,1)} %pad.4.low), custom_call_target="tpu_custom_call" | custom-call | tf_op jit(solution)/shard_map/gather_attended/pallas_call | solution.py:545
  195.4 3.6 %convolution_bitcast_fusion.2 = f32[384,256]{1,0:T(8,128)S(1)} fusion(bf16[16,384,256]{2,1,0:T(8,128)(2,1)} %get-tuple-element.14, bf16[16,256,256]{2,1,0:T(8,128)(2,1)} %get-tuple-element.15), kind=kOutput, calls=%fused_computation.17 | convolution fusion | flops 805306368 | bytes 5636096 | tf_op jit(solution)/shard_map/mgk,mck->gc/dot_general | solution.py:563
  199.0 0.9 fusion.8
  (36 shorter events, 0.2 us)
Async XLA Ops:
  0.6 13.0 %copy-start = (bf16[128,2,1024]{2,1,0:T(2,128)(2,1)S(1)}, bf16[128,2,1024]{2,1,0:T(2,128)(2,1)}, u32[]{:S(2)}) copy-start(bf16[128,2,1024]{2,1,0:T(2,128)(2,1)} %param.25) | copy-start | bytes 1572868
  1.6 126.1 %copy-start.11 = (f32[64]{0:T(128)}, f32[64]{0:T(128)S(1)}, u32[]{:S(2)}) copy-start(f32[64]{0:T(128)S(1)} %multiply_exponential_fusion) | copy-start | bytes 772
  121.7 8.1 %copy-start.1 = (bf16[32,320,256]{2,1,0:T(8,128)(2,1)S(1)}, bf16[32,320,256]{2,1,0:T(8,128)(2,1)}, u32[]{:S(2)}) copy-start(bf16[32,320,256]{2,1,0:T(8,128)(2,1)} %get-tuple-element.11) | copy-start | bytes 15728644
  121.7 8.1 %copy-start.2 = (bf16[32,64,256]{2,1,0:T(8,128)(2,1)S(1)}, bf16[32,64,256]{2,1,0:T(8,128)(2,1)}, u32[]{:S(2)}) copy-start(bf16[32,64,256]{2,1,0:T(8,128)(2,1)} %get-tuple-element.13) | copy-start | bytes 3145732
  137.7 4.9 %copy-start.8 = (s32[1024]{0:T(1024)S(1)}, s32[1024]{0:T(1024)}, u32[]{:S(2)}) copy-start(s32[1024]{0:T(1024)} %pad_clamp_fusion) | copy-start | bytes 12292
  137.8 7.0 %copy-start.10 = (pred[4]{0:T(512)(128)(4,1)S(1)}, pred[4]{0:T(512)(128)(4,1)}, u32[]{:S(2)}) copy-start(pred[4]{0:T(512)(128)(4,1)} %get-tuple-element.27) | copy-start | bytes 16
  150.6 5.0 %copy-start.7 = (bf16[384,16]{0,1:T(8,128)(2,1)S(1)}, bf16[384,16]{0,1:T(8,128)(2,1)}, u32[]{:S(2)}) copy-start(bf16[384,16]{0,1:T(8,128)(2,1)} %get-tuple-element.41) | copy-start | bytes 36868
  150.6 5.0 %copy-start.9 = (f32[384]{0:T(512)S(1)}, f32[384]{0:T(512)}, u32[]{:S(2)}) copy-start(f32[384]{0:T(512)} %add_rsqrt_fusion.2) | copy-start | bytes 4612
  150.6 5.9 %copy-start.13 = (f32[128]{0:T(128)S(1)}, f32[128]{0:T(128)}, u32[]{:S(2)}) copy-start(f32[128]{0:T(128)} %convert_element_type.110) | copy-start | bytes 1540
  150.6 6.0 %copy-start.12 = (f32[64]{0:T(128)S(1)}, f32[64]{0:T(128)}, u32[]{:S(2)}) copy-start(f32[64]{0:T(128)} %copy-done.11) | copy-start | bytes 772
  155.6 3.6 %copy-start.14 = (f32[128]{0:T(128)S(1)}, f32[128]{0:T(128)}, u32[]{:S(2)}) copy-start(f32[128]{0:T(128)} %convert_element_type.113) | copy-start | bytes 1540
  156.2 3.5 %copy-start.3 = (pred[384,896]{0,1:T(8,128)(4,1)S(1)}, pred[384,896]{0,1:T(8,128)(4,1)}, u32[]{:S(2)}) copy-start(pred[384,896]{0,1:T(8,128)(4,1)} %pad_add_fusion) | copy-start | bytes 1032196
  156.2 3.5 %copy-start.5 = (bf16[512,128]{1,0:T(8,128)(2,1)S(1)}, bf16[512,128]{1,0:T(8,128)(2,1)}, u32[]{:S(2)}) copy-start(bf16[512,128]{1,0:T(8,128)(2,1)} %get-tuple-element.54) | copy-start | bytes 393220
  159.4 1.2 copy-start.4
  195.4 3.6 %copy-start.6 = (bf16[16,32,384]{2,1,0:T(8,128)(2,1)S(1)}, bf16[16,32,384]{2,1,0:T(8,128)(2,1)}, u32[]{:S(2)}) copy-start(bf16[16,32,384]{2,1,0:T(8,128)(2,1)} %get-tuple-element.16) | copy-start | bytes 1179652

commit v2 on v1

v2 whole, which is shorter than its diff:
```python
import functools
import math

import jax
import jax.numpy as jnp
import numpy as np
from jax import lax
from jax.experimental import pallas as pl
from jax.experimental.pallas import tpu as pltpu
from jax.sharding import PartitionSpec as P

QUERY_HEADS = 32
KEY_VALUE_HEADS = 8
HEAD_SIZE = 128
ADAPTER_RANK = 16
PAGE = 64
MESH = pl.DeviceIdType.MESH

epsilon = 1e-06
rope_base = 1000000.0

Z_COUNT, NX, NY = 16, 4, 4
ROWS, COLS = 384, 256


class Links:
    def __init__(self, send, recv):
        self.send, self.recv, self.used, self.pending = send, recv, 0, []

    def start(self, src, dst, device):
        slot = self.used
        self.used += 1
        copy = pltpu.make_async_remote_copy(
            src_ref=src,
            dst_ref=dst,
            send_sem=self.send.at[slot],
            recv_sem=self.recv.at[slot],
            device_id=device,
            device_id_type=MESH,
        )
        copy.start()
        self.pending.append(copy)
        return copy

    def drain(self):
        for copy in self.pending:
            copy.wait_send()
        self.pending = []


class Place:
    def __init__(self):
        self.r = lax.axis_index("req")
        self.m = lax.axis_index("mlp")
        self.x = lax.rem(self.m, NX)
        self.y = lax.div(self.m, NX)

    def along(self, axis, step):
        if axis == "x":
            return self.m - self.x + lax.rem(self.x + (step + NX), NX)
        return lax.rem(self.m + (step + NY) * NX, NX * NY)

    def at(self, axis_a, i, axis_b, j):
        x = self.x + (i if axis_a == "x" else j) + NX
        y = self.y + (i if axis_a == "y" else j) + NY
        return lax.rem(y, NY) * NX + lax.rem(x, NX)


def barrier(place, whole_plane):
    sem = pltpu.get_barrier_semaphore()
    n = 0
    r, m = place.r, place.m
    for other in (lax.rem(r + 2, 32), lax.rem(r + 30, 32), r + 1 - 2 * lax.rem(r, 2)):
        pl.semaphore_signal(sem, inc=1, device_id=(other, m), device_id_type=MESH)
        n += 1
    for d in range(1, NX * NY):
        other = lax.rem(m + d, NX * NY)
        pl.semaphore_signal(sem, inc=1, device_id=(r, other), device_id_type=MESH)
        n += 1
    pl.semaphore_wait(sem, n)


class PlaneGather:
    def __init__(self, links, place, buf, rows):
        self.links, self.place, self.buf, self.rows = links, place, buf, rows
        self.p1, self.p2, self.q1, self.q2 = {}, {}, {}, {}
        self.axes = [("x", "y"), ("y", "x")]

    def view(self, h, piece, part=None):
        rows = self.rows // 2
        begin = h * rows
        if part is not None:
            rows //= 2
            begin += part * rows
        return self.buf.at[piece, pl.ds(begin, rows), :]

    def send(self, h, axis, step, piece, part=None):
        view = self.view(h, piece, part)
        return self.links.start(view, view, (self.place.r, self.place.along(axis, step)))

    def piece(self, h, i):
        a, b = self.axes[h]
        return self.place.at(a, i, b, 0)

    def start_second(self, h, i):
        b = self.axes[h][1]
        for s in (1, -1):
            self.q1[h, i, s] = self.send(h, b, s, self.piece(h, i))

    def e0(self):
        for h in range(2):
            a = self.axes[h][0]
            for s in (1, -1):
                self.p1[h, s] = self.send(h, a, s, self.place.m)
        for h in range(2):
            self.start_second(h, 0)

    def e1(self):
        for h in range(2):
            a = self.axes[h][0]
            for s in (1, -1):
                self.p1[h, s].wait_recv()
                self.p2[h, s] = self.send(h, a, s, self.piece(h, -s), 0 if s == 1 else 1)
        for h in range(2):
            for s in (1, -1):
                self.start_second(h, -s)

    def e2(self):
        for h in range(2):
            for s in (1, -1):
                self.p2[h, s].wait_recv()
            self.start_second(h, 2)

    def e3(self, i):
        for h in range(2):
            a, b = self.axes[h]
            for s in (1, -1):
                self.q1[h, i, s].wait_recv()
                piece = self.place.at(a, i, b, -s)
                self.q2[h, i, s] = self.send(h, b, s, piece, 0 if s == 1 else 1)

    def e4(self):
        for copy in self.q2.values():
            copy.wait_recv()

    def run(self):
        self.e0()
        self.e1()
        self.e2()
        for i in (0, -1, 1, 2):
            self.e3(i)
        self.e4()


class RingGather:
    def __init__(self, links, place, view, halves):
        self.links, self.place, self.view, self.halves = links, place, view, halves
        self.z, self.sib = {}, {}

    def shard(self, t):
        return lax.rem(self.place.r + (2 * t + 32), 32)

    def send(self, t, s):
        shard = self.shard(-s * t)
        target = (lax.rem(self.place.r + (2 * s + 32), 32), self.place.m)
        if t == Z_COUNT // 2 - 1:
            view = self.halves(shard, 0 if s == 1 else 1)
        else:
            view = self.view(shard)
        self.z[t, s] = self.links.start(view, view, target)

    def sibling(self, t):
        view = self.view(self.shard(t))
        r = self.place.r
        self.sib[t] = self.links.start(view, view, (r + 1 - 2 * lax.rem(r, 2), self.place.m))

    def step(self, t):
        last = Z_COUNT // 2
        if t == 0:
            for s in (1, -1):
                self.send(0, s)
            self.sibling(0)
            return
        for s in (1, -1):
            self.z[t - 1, s].wait_recv()
            if t < last:
                self.send(t, s)
        if t < last:
            for s in (1, -1):
                self.sibling(-s * t)
        else:
            self.sibling(last)

    def siblings(self, t):
        for i in {t, -t} if t < Z_COUNT // 2 else {t}:
            self.sib[i].wait_recv()

    def finish(self):
        for copy in self.sib.values():
            copy.wait_recv()


class Fused:
    def __init__(self, ins, outs, scratch):
        (
            self.lengths,
            self.prefix,
            self.pages,
            self.chosen,
            self.storage,
            self.hid,
            self.gain,
            self.head_gain,
            self.freq,
            self.down_qkv,
            self.wq,
            self.wkv,
            self.up_q,
            self.up_kv,
            self.down_out,
            self.up_out,
            self.wo,
            self.pool,
        ) = ins
        self.out, self.cache = outs
        (
            self.hid_all,
            self.scaled,
            self.down_all,
            self.mid_all,
            self.late_all,
            self.wo_all,
            self.low_all,
            self.att_all,
            self.low_out_all,
            self.cached,
            self.acc,
            self.sq,
            self.cos,
            self.sin,
            self.query,
            self.key,
            self.turned,
            self.pool_ok,
            send,
            recv,
            self.local,
        ) = scratch
        self.place = Place()
        self.r, self.m = self.place.r, self.place.m
        self.chip = lax.div(self.r, 2)
        self.links = Links(send, recv)
        links, place = self.links, self.place
        self.plane = PlaneGather(links, place, self.hid_all, ROWS)
        self.lows = PlaneGather(links, place, self.low_all, 64)
        self.att = PlaneGather(links, place, self.att_all, ROWS)
        self.low_outs = PlaneGather(links, place, self.low_out_all, 32)
        self.early = RingGather(links, place, *rows_of(self.down_all, 0, 96))
        self.mid = [
            RingGather(links, place, *rows_of(self.mid_all, begin, rows))
            for begin, rows in MID_PARTS
        ]
        self.late = RingGather(links, place, *rows_of(self.late_all, 0, 64))
        self.wide = RingGather(
            links,
            place,
            lambda shard: self.wo_all.at[:, pl.ds(shard * 8, 8), :],
            lambda shard, part: self.wo_all.at[pl.ds(8 * part, 8), pl.ds(shard * 8, 8), :],
        )


    def stage(self):
        r, m = self.r, self.m
        staged = []

        def move(src, dst):
            copy = pltpu.make_async_copy(src, dst, self.local.at[len(staged)])
            copy.start()
            staged.append(copy)

        for i in range(2):
            move(self.down_qkv.at[i], self.down_all.at[r, pl.ds(48 * i, 48), :])
        move(self.hid, self.hid_all.at[m])
        move(self.wq, self.mid_all.at[r, pl.ds(0, 128), :])
        move(self.wkv, self.mid_all.at[r, pl.ds(128, 128), :])
        for i in range(2):
            move(self.up_q.at[i], self.mid_all.at[r, pl.ds(256 + 16 * i, 16), :])
            move(self.up_kv.at[i], self.mid_all.at[r, pl.ds(288 + 16 * i, 16), :])
            move(self.down_out.at[i], self.late_all.at[r, pl.ds(16 * i, 16), :])
            move(self.up_out.at[i], self.late_all.at[r, pl.ds(32 + 16 * i, 16), :])
        move(self.wo.at[m], self.wo_all.at[m, pl.ds(r * 8, 8), :])
        move(self.pool, self.cached)
        return staged

    def swap(self):
        self.swaps = []
        for d in range(1, NX * NY):
            other = lax.rem(self.m + d, NX * NY)
            self.swaps.append(
                self.links.start(
                    self.wo.at[other],
                    self.wo_all.at[self.m, pl.ds(self.r * 8, 8), :],
                    (self.r, other),
                )
            )

    def ends(self):
        e1 = self.lengths[0, 0]
        e2 = e1 + self.lengths[0, 1]
        e3 = e2 + self.lengths[0, 2]
        return e1, e2, e3

    def owner(self, index):
        e1, e2, e3 = self.ends()
        return (
            (index >= e1).astype(jnp.int32)
            + (index >= e2).astype(jnp.int32)
            + (index >= e3).astype(jnp.int32)
        )

    def owner_lane(self):
        return self.owner(lax.broadcasted_iota(jnp.int32, (1, ROWS), 1))

    def owner_row(self, lanes):
        return self.owner(lax.broadcasted_iota(jnp.int32, (ROWS, lanes), 0))

    def tables(self):
        e1, e2, e3 = self.ends()
        row = lax.broadcasted_iota(jnp.int32, (ROWS, HEAD_SIZE), 0)
        owner = self.owner(row)
        shift = PAGE * self.prefix[0, 0] + jnp.zeros_like(row)
        for j, begin in ((1, e1), (2, e2), (3, e3)):
            shift = jnp.where(owner == j, PAGE * self.prefix[0, j] - begin, shift)
        angles = (row + shift).astype(jnp.float32) * self.freq[...]
        self.cos[...] = jnp.cos(angles)
        lane = lax.broadcasted_iota(jnp.int32, (ROWS, HEAD_SIZE), 1)
        sine = jnp.sin(angles)
        self.sin[...] = jnp.where(lane < HEAD_SIZE // 2, -sine, sine)

    def pool_mask(self):
        page = lax.div(lax.broadcasted_iota(jnp.int32, (1, 8 * PAGE), 1), PAGE)
        owner = self.owner_row(8 * PAGE)
        mask = jnp.zeros((ROWS, 8 * PAGE), jnp.float32)
        for j in range(4):
            used = jnp.zeros((1, 8 * PAGE), jnp.float32)
            count = self.prefix[0, j]
            for i in range(8):
                wanted = self.pages[j, i] + 64 * jnp.maximum(i + 1 - count, 0)
                used = jnp.where(page == wanted, 1.0, used)
            mask = jnp.where(owner == j, used, mask)
        self.pool_ok[...] = mask


    def slot(self, j):
        return self.storage[self.chosen[0, j]]

    def rows_at(self, ref, begin, rows, j):
        slot = self.slot(j)
        return ref[slot // 2, pl.ds(begin + (slot % 2) * rows, rows), :]

    def own_terms(self):
        scaled = (self.hid[...].astype(jnp.float32) * self.gain[pl.ds(self.m, 1), :]).astype(
            jnp.bfloat16
        )
        owner = self.owner_lane()
        low = jnp.zeros((48, ROWS), jnp.float32)
        for j in range(4):
            slot = self.slot(j)
            down = self.down_all[slot // 2, pl.ds((slot % 2) * 48, 48), :]
            terms = lax.dot_general(
                down, scaled, (((1,), (1,)), ((), ())), preferred_element_type=jnp.float32
            )
            low = low + jnp.where(owner == j, terms, 0.0)
        self.low_all[self.m, 0:48, :] = low.astype(jnp.bfloat16)
        self.low_all[self.m, 48:64, :] = jnp.zeros((16, ROWS), jnp.bfloat16)

    def scale_piece(self, i):
        h = self.hid_all[i].astype(jnp.float32)
        self.sq[...] += h * h
        self.scaled[i] = (h * self.gain[pl.ds(i, 1), :]).astype(jnp.bfloat16)

    def scale_all(self):
        self.sq[...] = jnp.zeros_like(self.sq)
        self.acc[...] = jnp.zeros_like(self.acc)

        def one(i, carry):
            self.scale_piece(i)
            return carry

        lax.fori_loop(0, 16, one, 0)

    def project(self, chip):
        x = self.scaled[chip]
        for part in range(2):
            w = jnp.concatenate(
                [
                    self.mid_all[2 * chip, pl.ds(128 * part, 128), :],
                    self.mid_all[2 * chip + 1, pl.ds(128 * part, 128), :],
                ],
                axis=0,
            )
            self.acc[part] += jnp.dot(x, w, preferred_element_type=jnp.float32)

    def project_step(self, t):
        chips = [self.chip] if t == 0 else [lax.rem(self.chip + t, 16)]
        if 0 < t < 8:
            chips.append(lax.rem(self.chip + 16 - t, 16))
        for chip in chips:
            self.project(chip)

    def masked_terms(self, low):
        owner = self.owner_lane()
        return jnp.concatenate([jnp.where(owner == j, low, 0.0) for j in range(4)], axis=0)

    def ups(self, ref, begin):
        return jnp.concatenate([self.rows_at(ref, begin, 16, j) for j in range(4)], axis=0)

    def head(self, values, gain_row):
        values = values.astype(jnp.bfloat16).astype(jnp.float32)
        mean_sq = jnp.mean(values * values, axis=-1, keepdims=True)
        values = values * lax.rsqrt(mean_sq + epsilon) * self.head_gain[gain_row : gain_row + 1, :]
        turned = pltpu.roll(values, HEAD_SIZE // 2, 1)
        return values * self.cos[...] + turned * self.sin[...]

    def finish_projection(self):
        low = jnp.zeros((48, ROWS), jnp.float32)
        for i in range(16):
            low = low + self.low_all[i, 0:48, :].astype(jnp.float32)
        up_q = self.ups(self.mid_all, 256)
        up_kv = self.ups(self.mid_all, 288)
        q_terms = self.masked_terms(low[0:16]).T.astype(jnp.bfloat16)
        k_terms = self.masked_terms(low[16:32]).T.astype(jnp.bfloat16)
        v_terms = self.masked_terms(low[32:48]).T.astype(jnp.bfloat16)
        scale = lax.rsqrt(jnp.sum(self.sq[...], axis=1, keepdims=True) / 4096.0 + epsilon)
        dot = functools.partial(jnp.dot, preferred_element_type=jnp.float32)
        query = scale * (self.acc[0] + dot(q_terms, up_q))
        key = scale * (self.acc[1, :, 0:128] + dot(k_terms, up_kv[:, 0:128]))
        value = scale * (self.acc[1, :, 128:256] + dot(v_terms, up_kv[:, 128:256]))
        for h in range(2):
            self.query[h] = self.head(query[:, 128 * h : 128 * h + 128], 0).astype(jnp.bfloat16)
        key = self.head(key, 1)
        value = value.astype(jnp.bfloat16)
        self.key[0] = key.astype(jnp.bfloat16)
        self.key[1] = value
        self.turned[0] = key.T
        self.turned[1] = value.astype(jnp.float32).T

    def store_cache(self):
        first = pl.multiple_of(lax.rem(self.m, 2) * 64, 64)
        for i in range(2):
            self.cache[i] = self.turned[i, pl.ds(first, 64), :].astype(jnp.bfloat16)

    def attend(self, h):
        query = self.query[h]
        nt = (((1,), (1,)), ((), ()))
        by = 1.0 / math.sqrt(HEAD_SIZE)

        def parts(keys, mask):
            scores = lax.dot_general(query, keys, nt, preferred_element_type=jnp.float32)
            return jnp.where(mask, jnp.exp(scores * by - 4.0), 0.0)

        old = parts(self.cached[:, 0:128], self.pool_ok[...] > 0.5)
        row = lax.broadcasted_iota(jnp.int32, (ROWS, ROWS), 0)
        lane = lax.broadcasted_iota(jnp.int32, (ROWS, ROWS), 1)
        seen = (self.owner(row) == self.owner_lane()) & (lane <= row)
        new = parts(self.key[0], seen)
        total = jnp.sum(old, axis=1, keepdims=True) + jnp.sum(new, axis=1, keepdims=True)
        values = jnp.dot(
            old.astype(jnp.bfloat16), self.cached[:, 128:256], preferred_element_type=jnp.float32
        ) + jnp.dot(new.astype(jnp.bfloat16), self.key[1], preferred_element_type=jnp.float32)
        self.att_all[self.m, :, 128 * h : 128 * h + 128] = (values / total).astype(jnp.bfloat16)

    def own_output_terms(self):
        downs = self.ups(self.late_all, 0)
        terms = lax.dot_general(
            downs,
            self.att_all[self.m],
            (((1,), (1,)), ((), ())),
            preferred_element_type=jnp.float32,
        )
        owner = self.owner_lane()
        low = jnp.zeros((16, ROWS), jnp.float32)
        for j in range(4):
            low = low + jnp.where(owner == j, terms[16 * j : 16 * j + 16], 0.0)
        self.low_out_all[self.m, 0:16, :] = low.astype(jnp.bfloat16)
        self.low_out_all[self.m, 16:32, :] = jnp.zeros((16, ROWS), jnp.bfloat16)

    def output_piece(self, piece, first=False):
        update = lax.dot_general(
            self.att_all[piece],
            self.wo_all[piece],
            (((1,), (1,)), ((), ())),
            preferred_element_type=jnp.float32,
        )
        if first:
            self.acc[0] = update
        else:
            self.acc[0] += update

    def finish_output(self):
        low = jnp.zeros((16, ROWS), jnp.float32)
        for i in range(16):
            low = low + self.low_out_all[i, 0:16, :].astype(jnp.float32)
        terms = self.masked_terms(low).T.astype(jnp.bfloat16)
        update = jnp.dot(terms, self.ups(self.late_all, 32), preferred_element_type=jnp.float32)
        self.out[...] = (self.acc[0] + update).astype(jnp.bfloat16)

    def late_step(self, t):
        self.late.step(t)
        self.wide.step(t)

    def mid_step(self, t):
        for ring in self.mid:
            ring.step(t)

    def mid_siblings(self, t):
        for ring in self.mid:
            ring.siblings(t)


def rows_of(ref, begin, rows):
    return (
        lambda shard: ref.at[shard, pl.ds(begin, rows), :],
        lambda shard, part: ref.at[shard, pl.ds(begin + part * (rows // 2), rows // 2), :],
    )


MID_PARTS = ((0, 160), (160, 160))


def layer_kernel(*refs):
    f = Fused(refs[:18], refs[18:20], refs[20:])
    staged = f.stage()
    barrier(f.place, True)
    for copy in staged:
        copy.wait()

    f.early.step(0)
    f.plane.e0()
    f.mid_step(0)
    f.swap()
    f.tables()
    f.early.step(1)
    f.plane.e1()
    f.mid_step(1)
    f.pool_mask()
    f.early.step(2)
    f.plane.e2()
    f.mid_step(2)
    f.early.step(3)
    f.plane.e3(0)
    f.mid_step(3)
    f.early.step(4)
    f.plane.e3(-1)
    f.plane.e3(1)
    f.mid_step(4)
    for copy in f.swaps:
        copy.wait_recv()
    f.late_step(0)
    f.early.step(5)
    f.plane.e3(2)
    f.mid_step(5)
    f.early.step(6)
    f.plane.e4()
    f.mid_step(6)
    f.scale_all()
    f.early.step(7)
    f.mid_step(7)
    f.late_step(1)
    f.early.step(8)
    f.early.finish()
    f.own_terms()
    f.lows.e0()
    for t in range(4):
        f.mid_siblings(t)
        f.project_step(t)
    f.lows.e1()
    f.mid_step(8)
    f.late_step(2)
    f.lows.e2()
    for t in range(4, 7):
        f.mid_siblings(t)
        f.project_step(t)
    for i in (0, -1, 1, 2):
        f.lows.e3(i)
    f.late_step(3)
    for t in range(7, 9):
        f.mid_siblings(t)
        f.project_step(t)
    f.lows.e4()
    f.finish_projection()
    f.late_step(4)
    f.attend(0)
    f.late_step(5)
    f.attend(1)
    f.att.e0()
    f.late_step(6)
    f.store_cache()
    f.att.e1()
    f.late_step(7)
    f.att.e2()
    f.late_step(8)
    f.late.finish()
    f.wide.finish()
    f.own_output_terms()
    f.low_outs.e0()
    f.output_piece(f.m, True)
    f.att.e3(0)
    f.att.e3(-1)
    f.low_outs.e1()
    f.att.e3(1)
    f.low_outs.e2()
    f.att.e3(2)
    for i in (0, -1, 1, 2):
        f.low_outs.e3(i)
    f.att.e4()
    for d in range(1, 16):
        f.output_piece(lax.rem(f.m + d, 16))
    f.low_outs.e4()
    f.finish_output()
    f.links.drain()


def shards(
    hidden_input,
    input_norm_gain,
    query_norm_gain,
    key_norm_gain,
    query_weight,
    key_value_weight,
    output_weight,
    adapter_down_qkv,
    adapter_down_output,
    adapter_up_query,
    adapter_up_key_value,
    adapter_up_output,
    pool,
    lengths,
    cached_prefix_pages,
    prefix_page_table,
    adapter_of_request,
    adapter_storage,
):
    mi = lax.axis_index("mlp")
    begin = mi // 2 * HEAD_SIZE
    bf16, f32 = jnp.bfloat16, jnp.float32
    own_wkv = lax.dynamic_slice_in_dim(key_value_weight, begin, HEAD_SIZE, 2).reshape(128, 256)
    own_ukv = lax.dynamic_slice_in_dim(adapter_up_key_value, begin, HEAD_SIZE, 3).reshape(2, 16, 256)
    cached = lax.dynamic_slice_in_dim(pool, begin, HEAD_SIZE, 2).reshape(512, 256)
    half = HEAD_SIZE // 2
    freq = np.exp(
        np.arange(half, dtype=np.float32) * np.float32(-2.0 / HEAD_SIZE) * np.float32(math.log(rope_base))
    ).astype(np.float32)
    freq = np.concatenate([freq, freq])[None, :]

    smem = pl.BlockSpec(memory_space=pltpu.SMEM)
    vmem = pl.BlockSpec(memory_space=pltpu.VMEM)
    hbm = pl.BlockSpec(memory_space=pl.ANY)
    sems = 360
    update, cache = pl.pallas_call(
        layer_kernel,
        out_shape=(
            jax.ShapeDtypeStruct((ROWS, COLS), bf16),
            jax.ShapeDtypeStruct((2, 64, ROWS), bf16),
        ),
        in_specs=[smem] * 5 + [vmem] * 4 + [hbm] * 9,
        out_specs=(vmem, vmem),
        scratch_shapes=[
            pltpu.VMEM((16, ROWS, COLS), bf16),
            pltpu.VMEM((16, ROWS, COLS), bf16),
            pltpu.VMEM((32, 96, COLS), bf16),
            pltpu.VMEM((32, 320, COLS), bf16),
            pltpu.VMEM((32, 64, COLS), bf16),
            pltpu.VMEM((16, 256, COLS), bf16),
            pltpu.VMEM((16, 64, ROWS), bf16),
            pltpu.VMEM((16, ROWS, COLS), bf16),
            pltpu.VMEM((16, 32, ROWS), bf16),
            pltpu.VMEM((512, COLS), bf16),
            pltpu.VMEM((2, ROWS, COLS), f32),
            pltpu.VMEM((ROWS, COLS), f32),
            pltpu.VMEM((ROWS, HEAD_SIZE), f32),
            pltpu.VMEM((ROWS, HEAD_SIZE), f32),
            pltpu.VMEM((2, ROWS, HEAD_SIZE), bf16),
            pltpu.VMEM((2, ROWS, HEAD_SIZE), bf16),
            pltpu.VMEM((2, HEAD_SIZE, ROWS), f32),
            pltpu.VMEM((ROWS, 8 * PAGE), f32),
            pltpu.SemaphoreType.DMA((sems,)),
            pltpu.SemaphoreType.DMA((sems,)),
            pltpu.SemaphoreType.DMA((16,)),
        ],
        compiler_params=pltpu.CompilerParams(
            collective_id=0, has_side_effects=True, vmem_limit_bytes=56 * 2**20
        ),
        name="layer",
    )(
        lengths,
        cached_prefix_pages,
        prefix_page_table.reshape(4, 8),
        adapter_of_request.reshape(1, 4),
        adapter_storage,
        hidden_input,
        input_norm_gain.astype(f32).reshape(16, COLS),
        jnp.stack([query_norm_gain, key_norm_gain]).astype(f32),
        freq,
        adapter_down_qkv,
        query_weight,
        own_wkv,
        adapter_up_query,
        own_ukv,
        adapter_down_output,
        adapter_up_output,
        jnp.transpose(output_weight, (1, 2, 0)),
        cached,
    )
    return (update, jnp.transpose(cache, (2, 0, 1)))


def solution(mesh):
    return jax.shard_map(
        shards,
        mesh=mesh,
        in_specs=(
            P("req", "mlp"),
            P(),
            P(),
            P(),
            P("req", "mlp"),
            P("req", None, None),
            P("mlp", None, "req"),
            P("req", None, "mlp"),
            P("req", None, "mlp"),
            P("req", None, "mlp"),
            P("req", None, None, None),
            P("req", None, "mlp"),
            P("req", None, None),
            P("req", None),
            P("req", None),
            P("req", None, None),
            P("req", None, None),
            P(),
        ),
        out_specs=(P("req", "mlp"), P("req", None, "mlp")),
        check_vma=False,
    )
```

time: 201 us -> 115 us (0.57)
  Pallas kernels: 135 us -> 105 us
  local copies, waits for them, and re-layouts: 30.8 us -> 8.25 us
  other arithmetic: 20.1 us -> 1.4 us
  matrix products: 12.6 us -> 0 us
    pallas_call x2 -> x1, Pallas kernels: 135 us -> 105 us  [shards(): pl.pallas_call(layer_kernel, out_shape=(jax.ShapeDtypeStruct((ROWS, COLS)...]
    dot_general x10 -> x0, matrix products: 12.6 us -> none  [the longest x1 4.96 us: shards(): total = jnp.dot(wide, weights, preferred_element_type=jnp.float32)]
    reduce_sum x6 -> x0, other arithmetic: 7.42 us -> none  [the longest x1 5.97 us: shards(): jnp.sum(hid32 * hid32, axis=(0, 2)) / 4096.0 + epsilon]
    reshape x4 -> x1, local copies, waits for them, and re-layouts: 8.09 us -> 1.31 us  [shards(): input_norm_gain.astype(f32).reshape(16, COLS)]
    transpose x1 -> x0, local copies, waits for them, and re-layouts: 4.66 us -> none  [shards(): wide = jnp.transpose(scaled, (1, 0, 2)).reshape(ROWS, 4096)]
    gather x5 -> x0, local copies, waits for them, and re-layouts: 4.53 us -> none  [the longest x1 1.59 us: shards(): jnp.take(mid_all[:, 256:288].reshape(64, 16, 256), slot_indices, axis=0)]
    slice x4 -> x0, local copies, waits for them, and re-layouts: 3.63 us -> none  [the longest x1 1.62 us: shards(): value_matrix = jnp.concatenate([cached[:, 1], value_plain], axis=0)]
    convert_element_type x7 -> x1, other arithmetic: 4.1 us -> 1.4 us  [shards(): jnp.stack([query_norm_gain, key_norm_gain]).astype(f32)]
where the time goes in v2:
time: 115 us
  Pallas kernels  105 us (91%)
  local copies, waits for them, and re-layouts  8.25 us (7%)
  other arithmetic  1.4 us (1%)
    pallas_call x1, Pallas kernels, shards(): pl.pallas_call(layer_kernel, out_shape=(jax.ShapeDtypeStruct((ROWS, COLS)...  105 us
    unnamed x6, local copies, waits for them, and re-layouts  4.53 us

profile of v2, /device:TPU:1, one launch (start us, length us, event | category | flops | bytes accessed | tf_op | source)
XLA Modules:
  0.0 114.9 jit_solution(2462317868468617232)
XLA Ops:
  0.6 0.0 copy-start
  0.7 1.4 %maximum_convert_fusion.refs_7_ = f32[2,128]{1,0:T(2,128)} fusion(bf16[1,128]{1,0:T(2,128)(2,1)} %bitcast.21, bf16[1,128]{1,0:T(2,128)(2,1)} %bitcast.22), kind=kLoop, calls=%fused_computation.5 | loop fusion | flops 1024 | bytes 1536 | tf_op jit(solution)/shard_map/convert_element_type | solution.py:703
  2.1 1.3 %reshape.32.refs_6_ = f32[16,256]{1,0:T(8,128)} reshape(bf16[4096]{0:T(1024)(128)(2,1)} %param.20) | data formatting | bytes 24576 | tf_op jit(solution)/shard_map/reshape | solution.py:702
  3.4 0.7 constant_dynamic-slice_fusion.1
  4.1 0.6 reshape.29.refs_13_
  4.7 0.9 constant_dynamic-slice_fusion.2
  5.6 0.6 copy.26
  6.2 0.0 copy-done
  6.2 0.2 constant_dynamic-slice_fusion
  6.4 0.7 copy.25
  7.2 104.5 %layer.1 = (bf16[384,256]{1,0:T(8,128)(2,1)}, bf16[2,64,384]{2,1,0:T(8,128)(2,1)}) custom-call(s32[1,4]{1,0:T(1,128)} %refs_0_.1, s32[1,4]{1,0:T(1,128)} %refs_1_.1, s32[4,8]{1,0:T(4,128)} %bitcast.20, s32[1,4]{1,0:T(1,128)} %bitcast.23, s32[64]{0:T(128)} %refs_4_.1, bf16[384,256]{1,0:T(8,128)(2,1)} %refs_5_.1, f32[16,256]{1,0:T(8,128)} %reshape.32.refs_6_, ...), custom_call_target="tpu_custom_call" | custom-call | tf_op jit(solution)/shard_map/layer/pallas_call | solution.py:660
  111.7 1.6 %copy.29 = bf16[384,256]{1,0:T(8,128)(2,1)} copy(bf16[384,256]{1,0:T(8,128)(2,1)} %get-tuple-element.8) | data formatting | bytes 393216
  113.3 1.5 %copy.30 = bf16[384,2,64]{0,2,1:T(8,128)(2,1)} copy(bf16[384,2,64]{0,2,1:T(8,128)(2,1)} %bitcast.18) | data formatting | bytes 196608
Async XLA Ops:
  0.6 5.6 %copy-start = (bf16[512,2,1024]{2,1,0:T(2,128)(2,1)S(1)}, bf16[512,2,1024]{2,1,0:T(2,128)(2,1)}, u32[]{:S(2)}) copy-start(bf16[512,2,1024]{2,1,0:T(2,128)(2,1)} %param.31) | copy-start | bytes 6291460
